TPU v7x, 128 devices: a whole 4x4x4 slice. The times are simulated.
128 devices in a mesh: req: 16 (over y, z), tp: 8 (over x, core).
Axes of the slice: x: 4, y: 4, z: 4, core: 2. Of those that a mesh axis runs over, the one named last changes fastest.
Arguments:
- short_tokens: bfloat16 [1536, 3072], P('req')
- long_tokens: bfloat16 [8, 3072], replicated
- norm_gain: bfloat16 [3072], replicated, may hold values from 0.5 to 1.5
- w_query: bfloat16 [3072, 3072], P(None, 'tp'), may hold values from -0.109375 to 0.109375
- w_key: bfloat16 [3072, 1024], P(None, 'tp'), may hold values from -0.109375 to 0.109375
- w_value: bfloat16 [3072, 1024], P(None, 'tp'), may hold values from -0.109375 to 0.109375
- w_out: bfloat16 [3072, 3072], P('tp'), may hold values from -0.109375 to 0.109375
- short_lengths: int32 [1536], P('req'), may hold values from 0 to 127
- long_lengths: int32 [8], replicated, may hold values from 6144 to 8191
- short_cache: bfloat16 [1536, 8, 128, 256], P('req', 'tp'), may hold values from -120 to 120
- long_cache: bfloat16 [8, 8, 8192, 256], P(None, 'tp', 'req'), may hold values from -120 to 120
Outputs:
- short_hidden: bfloat16 [1536, 3072], P('req')
- long_hidden: bfloat16 [8, 3072], replicated
- short_cache_new: bfloat16 [1536, 8, 128, 256], P('req', 'tp')
- long_cache_new: bfloat16 [8, 8, 8192, 256], P(None, 'tp', 'req')
All inputs are finite; a program needn't handle non-finite values.
Results may differ from a plain program's by a relative error of at most 0.0095.
Values may be sent and summed in bfloat16 or wider, within the bound.
A program may use at most 128 MiB of HBM per device.

v0:
```python
import jax
import jax.numpy as jnp
from jax import lax
from jax.sharding import PartitionSpec as P

rope_theta = 500000.0
floor_score = -1e30


def merged(value, axis, join):
    pieces = jax.tree.map(lambda part: lax.all_gather(part, axis), value)
    head = jax.tree.map(lambda part: part[0], pieces)
    tail = jax.tree.map(lambda part: part[1:], pieces)
    total, _ = lax.scan(lambda total, slab: (join(total, slab), None), head, tail)
    return total


def rotate(values, positions):
    half = values.shape[-1] // 2
    freq = rope_theta ** (-(jnp.arange(half, dtype=jnp.float32) * 2.0 / values.shape[-1]))
    angle = positions.astype(jnp.float32)[:, None] * freq[None, :]
    cosine = jnp.cos(angle)[:, None, :]
    sine = jnp.sin(angle)[:, None, :]
    front = values[..., :half]
    back = values[..., half:]
    return jnp.concatenate([front * cosine - back * sine, back * cosine + front * sine], axis=-1)


def join_partials(earlier, later):
    peak_one, total_one, summed_one = earlier
    peak_two, total_two, summed_two = later
    peak_new = jnp.maximum(peak_one, peak_two)
    factor_one = jnp.exp(peak_one - peak_new)
    factor_two = jnp.exp(peak_two - peak_new)
    total_new = total_one * factor_one + total_two * factor_two
    summed_new = summed_one * factor_one[..., None] + summed_two * factor_two[..., None]
    return (peak_new, total_new, summed_new)


def per_device(
    short_tokens,
    long_tokens,
    norm_gain,
    w_query,
    w_key,
    w_value,
    w_out,
    short_lengths,
    long_lengths,
    short_cache,
    long_cache,
):
    head_size = short_cache.shape[-1] // 2
    kv_local = short_cache.shape[1]
    short_count = short_tokens.shape[0]
    long_count = long_tokens.shape[0]
    all_tokens = jnp.concatenate([short_tokens, long_tokens], axis=0)
    positions = jnp.concatenate([short_lengths, long_lengths], axis=0)
    total_rows = all_tokens.shape[0]
    residual = all_tokens.astype(jnp.float32)
    normed = (
        residual
        * lax.rsqrt(jnp.mean(residual * residual, axis=-1, keepdims=True) + 1e-05)
        * norm_gain.astype(jnp.float32)
    ).astype(jnp.bfloat16)
    query = jnp.dot(normed, w_query, preferred_element_type=jnp.float32).reshape(
        total_rows, -1, head_size
    )
    group_size = query.shape[1] // kv_local
    query = (
        rotate(query, positions)
        .astype(jnp.bfloat16)
        .reshape(total_rows, kv_local, group_size, head_size)
    )
    key_new = jnp.dot(normed, w_key, preferred_element_type=jnp.float32).reshape(
        total_rows, kv_local, head_size
    )
    key_new = rotate(key_new, positions).astype(jnp.bfloat16)
    value_new = (
        jnp.dot(normed, w_value, preferred_element_type=jnp.float32)
        .reshape(total_rows, kv_local, head_size)
        .astype(jnp.bfloat16)
    )
    fresh = jnp.concatenate([key_new, value_new], axis=-1)
    score_scale = 1.0 / jnp.sqrt(jnp.float32(head_size))
    short_slots = jnp.arange(short_cache.shape[2], dtype=jnp.int32)
    short_write = short_slots[None, :] == short_lengths[:, None]
    short_out = jnp.where(
        short_write[:, None, :, None], fresh[:short_count, :, None, :], short_cache
    )
    short_scores = (
        jnp.einsum(
            "rkgd,rksd->rkgs",
            query[:short_count],
            short_out[..., :head_size],
            preferred_element_type=jnp.float32,
        )
        * score_scale
    )
    short_valid = (short_slots[None, :] <= short_lengths[:, None])[:, None, None, :]
    short_scores = jnp.where(short_valid, short_scores, floor_score)
    short_top = jnp.max(short_scores, axis=-1, keepdims=True)
    short_expo = jnp.where(short_valid, jnp.exp(short_scores - short_top), 0.0)
    short_weights = (short_expo / jnp.sum(short_expo, axis=-1, keepdims=True)).astype(jnp.bfloat16)
    short_mix = jnp.einsum(
        "rkgs,rksd->rkgd",
        short_weights,
        short_out[..., head_size:],
        preferred_element_type=jnp.float32,
    )
    span = long_cache.shape[2]
    first_slot = lax.axis_index("req") * span
    long_slots = first_slot + jnp.arange(span, dtype=jnp.int32)
    long_write = long_slots[None, :] == long_lengths[:, None]
    long_out = jnp.where(long_write[:, None, :, None], fresh[short_count:, :, None, :], long_cache)
    long_scores = (
        jnp.einsum(
            "lkgd,lksd->lkgs",
            query[short_count:],
            long_out[..., :head_size],
            preferred_element_type=jnp.float32,
        )
        * score_scale
    )
    long_valid = (long_slots[None, :] <= long_lengths[:, None])[:, None, None, :]
    long_scores = jnp.where(long_valid, long_scores, floor_score)
    long_peak = jnp.max(long_scores, axis=-1)
    long_expo = jnp.where(long_valid, jnp.exp(long_scores - long_peak[..., None]), 0.0)
    long_total = jnp.sum(long_expo, axis=-1)
    long_summed = jnp.einsum(
        "lkgs,lksd->lkgd",
        long_expo,
        long_out[..., head_size:].astype(jnp.float32),
        precision=lax.Precision.HIGHEST,
    )
    peak_all, total_all, summed_all = merged(
        (long_peak, long_total, long_summed), "req", join_partials
    )
    long_mix = summed_all / total_all[..., None]
    mixed = jnp.concatenate(
        [short_mix.reshape(short_count, -1), long_mix.reshape(long_count, -1)], axis=0
    ).astype(jnp.bfloat16)
    head_terms = jnp.dot(mixed, w_out, preferred_element_type=jnp.float32)
    summed_heads = lax.psum(head_terms, "tp")
    hidden = (residual + summed_heads).astype(jnp.bfloat16)
    return (hidden[:short_count], hidden[short_count:], short_out, long_out)


def solution(mesh):
    placed = (
        P("req", None),
        P(),
        P(),
        P(None, "tp"),
        P(None, "tp"),
        P(None, "tp"),
        P("tp", None),
        P("req"),
        P(),
        P("req", "tp", None, None),
        P(None, "tp", "req", None),
    )
    return jax.shard_map(
        per_device,
        mesh=mesh,
        in_specs=placed,
        out_specs=(P("req", None), P(), P("req", "tp", None, None), P(None, "tp", "req", None)),
        check_vma=False,
    )
```

profile of v0, /device:TPU:0, one launch (start us, length us, event | category | flops | bytes accessed | tf_op | source)
XLA Modules:
  0.0 178.5 jit_solution(13294808918669247572)
XLA Ops:
  7.3 0.8 convert_element_type.43
  8.1 1.4 fusion.7
  9.5 0.7 iota_compare_fusion.1
  10.3 0.8 add_convert_fusion.1
  11.0 0.9 multiply_cosine_fusion.1
  11.9 1.9 %convolution_bitcast_fusion = f32[104,1,128]{2,0,1:T(8,128)S(1)} fusion(bf16[3072,128]{1,0:T(8,128)(2,1)} %param.17, f32[3072]{0:T(1024)S(1)} %convert_element_type.43, f32[104]{0:T(128)S(1)} %add_rsqrt_fusion, bf16[8,3072]{1,0:T(8,128)(2,1)} %param.14, bf16[96,3072]{1,0:T(8,128)(2,1)} %param.13), kind=kOutput, calls=%fused_computation.33 | convolution fusion | flops 84025344 | bytes 1491360 | tf_op jit(solution)/shard_map/dot_general | solution.py:75
  13.8 0.3 fusion.30
  14.1 0.4 fusion.18
  14.5 0.7 pad_maximum_fusion.2
  15.3 1.1 fusion.43
  16.5 0.1 copy.64
  16.6 0.1 copy.65
  16.7 0.7 broadcast_compare_fusion.1
  17.5 1.9 %bitcast_select_fusion.1 = bf16[8,1,512,256]{3,2,0,1:T(8,128)(2,1)S(1)} fusion(bf16[8,1,512,256]{3,2,1,0:T(8,128)(2,1)} %param.23, pred[8,512]{1,0:T(8,128)(4,1)S(1)} %get-tuple-element.102, bf16[8,256]{1,0:T(8,128)(2,1)S(1)} %maximum_bitcast_fusion), kind=kLoop, calls=%fused_computation.17 | loop fusion | flops 1048576 | bytes 4202496 | tf_op jit(solution)/shard_map/jit(_where)/select_n | solution.py:115
  19.4 0.1 subtract_convert_fusion
  19.6 0.5 fusion.47
  20.1 0.6 fusion.19
  20.7 25.5 %all-gather.2 = f32[128,3,128]{2,0,1:T(8,128)S(1)} all-gather(f32[8,3,128]{2,0,1:T(8,128)S(1)} %copy.51), channel_id=4, replica_groups=mesh['req'=16,'tp'=8] {'req'}, dimensions={0}, use_global_device_ids=true | all-gather | bytes 208896 | tf_op jit(solution)/shard_map/all_gather | solution.py:11
  46.2 0.2 fusion.33
  46.4 0.1 copy.50
  46.5 22.8 %all-gather.4 = f32[16,8,3]{1,2,0:T(4,128)S(1)} all-gather(f32[1,8,3]{1,2,0:T(4,128)S(1)} %bitcast.102), channel_id=3, replica_groups=mesh['req'=16,'tp'=8] {'req'}, dimensions={0}, use_global_device_ids=true | all-gather | bytes 1632 | tf_op jit(solution)/shard_map/all_gather | solution.py:11
  69.3 0.1 copy.49
  69.4 21.1 %all-gather.3 = f32[16,8,3]{1,2,0:T(4,128)S(1)} all-gather(f32[1,8,3]{1,2,0:T(4,128)S(1)} %bitcast.103), channel_id=2, replica_groups=mesh['req'=16,'tp'=8] {'req'}, dimensions={0}, use_global_device_ids=true | all-gather | bytes 1632 | tf_op jit(solution)/shard_map/all_gather | solution.py:11
  90.5 6.2 %bitcast_select_fusion = bf16[96,1,128,256]{3,2,0,1:T(8,128)(2,1)S(1)} fusion(bf16[96,1,128,256]{3,2,1,0:T(8,128)(2,1)} %param.22, pred[96,128]{1,0:T(8,128)(4,1)S(1)} %get-tuple-element.106, bf16[96,256]{1,0:T(8,128)(2,1)S(1)} %slice_bitcast_fusion.15), kind=kLoop, calls=%fused_computation.12 | loop fusion | flops 3145728 | bytes 12644352 | tf_op jit(solution)/shard_map/jit(_where)/select_n | solution.py:88
  96.7 1.8 fusion.15
  98.5 0.3 fusion.48
  98.8 1.0 fusion.16
  99.9 4.6 %while.14 = (s32[]{:T(128)}, f32[8,1,3]{0,1,2:T(1,128)S(1)}, f32[8,1,3]{0,1,2:T(1,128)S(1)}, f32[8,1,3,128]{3,2,1,0:T(4,128)S(1)}, f32[15,8,1,3]{1,0,3,2:T(8,128...) while((s32[]{:T(128)}, f32[8,1,3]{0,1,2:T(1,128)S(1)}, ...), condition=%wide.region_6.7_spmd, body=%wide.region_5.6_spmd.sunk | while | flops 9362 | bytes 62877 | solution.py:14
  100.0 0.1 copy.85
  100.1 0.1 fusion.59
  100.3 0.1 copy.85
  100.4 0.1 fusion.59
  100.6 0.1 copy.85
  100.7 0.1 fusion.59
  100.9 0.1 copy.85
  101.1 0.1 fusion.59
  101.2 0.1 copy.85
  101.4 0.1 fusion.59
  101.5 0.1 copy.85
  101.7 0.1 fusion.59
  101.8 0.1 copy.85
  102.0 0.1 fusion.59
  102.1 0.1 copy.85
  102.3 0.1 fusion.59
  102.4 0.1 copy.85
  102.6 0.1 fusion.59
  102.7 0.1 copy.85
  102.9 0.1 fusion.59
  103.0 0.1 copy.85
  103.2 0.1 fusion.59
  103.3 0.1 copy.85
  103.5 0.1 fusion.59
  103.8 0.1 fusion.59
  104.0 0.1 copy.85
  104.1 0.1 fusion.59
  104.3 0.1 copy.85
  104.4 0.1 fusion.59
  104.6 1.6 fusion.21
  106.2 2.9 %fusion.54 = bf16[8,1,512,256]{3,2,1,0:T(8,128)(2,1)} fusion(bf16[8,1,512,256]{3,2,1,0:T(8,128)(2,1)} %param.23, bf16[8,256]{1,0:T(8,128)(2,1)S(1)} %maximum_bitcast_fusion, pred[8,512]{1,0:T(8,128)(4,1)S(1)} %get-tuple-element.102), kind=kLoop, calls=%fused_computation.92 | loop fusion | flops 1048576 | bytes 4202496
  109.1 7.6 %fusion.55 = bf16[96,1,128,256]{3,2,1,0:T(8,128)(2,1)} fusion(bf16[96,1,128,256]{3,2,1,0:T(8,128)(2,1)} %param.22, bf16[96,256]{1,0:T(8,128)(2,1)S(1)} %slice_bitcast_fusion.15, pred[96,128]{1,0:T(8,128)(4,1)S(1)} %get-tuple-element.106), kind=kLoop, calls=%fused_computation.93 | loop fusion | flops 3145728 | bytes 12644352
  116.7 52.1 %all-reduce.2.cloned.1.call-done = f32[104,3072]{1,0:T(8,128)} async-done(((f32[104,3072]{1,0:T(8,128)}), f32[104,3072]{1,0:T(8,128)}) %all-reduce.2.cloned.1.call-update) | async-done | bytes 1277968 | tf_op jit(solution)/shard_map/psum | solution.py:144
  168.8 1.4 fusion.10
  170.2 0.9 slice.107
  171.1 0.6 slice.108
  (99 shorter events, 2.2 us)
Async XLA Ops:
  7.2 97.5 %copy-start = (bf16[384,3072]{1,0:T(8,128)(2,1)S(1)}, bf16[384,3072]{1,0:T(8,128)(2,1)}, u32[]{:S(2)}) copy-start(bf16[384,3072]{1,0:T(8,128)(2,1)} %param.19) | copy-start | bytes 7077892
  7.2 6.9 %copy-start.1 = (bf16[96,3072]{1,0:T(8,128)(2,1)S(1)}, bf16[96,3072]{1,0:T(8,128)(2,1)}, u32[]{:S(2)}) copy-start(bf16[96,3072]{1,0:T(8,128)(2,1)} %param.13) | copy-start | bytes 1769476
  7.2 6.9 %copy-start.4 = (bf16[8,3072]{1,0:T(8,128)(2,1)S(1)}, bf16[8,3072]{1,0:T(8,128)(2,1)}, u32[]{:S(2)}) copy-start(bf16[8,3072]{1,0:T(8,128)(2,1)} %param.14) | copy-start | bytes 147460
  7.2 161.6 %all-reduce.2.cloned.1.call-start = ((), (), s32[]{:S(2)}) async-start(), calls=%async_computation | async-start | bytes 2555904 | tf_op jit(solution)/shard_map/psum | solution.py:144
  7.2 6.9 %copy-start.13 = (bf16[3072,128]{1,0:T(8,128)(2,1)S(1)}, bf16[3072,128]{1,0:T(8,128)(2,1)}, u32[]{:S(2)}) copy-start(bf16[3072,128]{1,0:T(8,128)(2,1)} %param.18) | copy-start | bytes 2359300
  11.9 3.4 %copy-start.12 = (bf16[3072,384]{1,0:T(8,128)(2,1)S(1)}, bf16[3072,384]{1,0:T(8,128)(2,1)}, u32[]{:S(2)}) copy-start(bf16[3072,384]{1,0:T(8,128)(2,1)} %param.16) | copy-start | bytes 7077892
  17.5 2.0 %copy-start.2 = (f32[104,64]{1,0:T(8,128)S(1)}, f32[104,64]{1,0:T(8,128)}, u32[]{:S(2)}) copy-start(f32[104,64]{1,0:T(8,128)} %get-tuple-element.104) | copy-start | bytes 79876
  19.6 26.6 %copy-start.8 = (bf16[104,3,64]{2,1,0:T(4,128)(2,1)}, bf16[104,3,64]{2,1,0:T(4,128)(2,1)S(1)}, u32[]{:S(2)}) copy-start(bf16[104,3,64]{2,1,0:T(4,128)(2,1)S(1)} %get-tuple-element.95) | copy-start | bytes 119812
  19.6 26.6 %copy-start.10 = (bf16[104,3,64]{2,1,0:T(4,128)(2,1)}, bf16[104,3,64]{2,1,0:T(4,128)(2,1)S(1)}, u32[]{:S(2)}) copy-start(bf16[104,3,64]{2,1,0:T(4,128)(2,1)S(1)} %get-tuple-element.96) | copy-start | bytes 119812
  19.6 70.9 %copy-start.3 = (bf16[104,1,256]{2,0,1:T(8,128)(2,1)S(1)}, bf16[104,1,256]{2,0,1:T(8,128)(2,1)}, u32[]{:S(2)}) copy-start(bf16[104,1,256]{2,0,1:T(8,128)(2,1)} %pad_maximum_fusion.2) | copy-start | bytes 159748
  69.3 27.4 %copy-start.6 = (f32[16,8,3]{1,2,0:T(4,128)}, f32[16,8,3]{1,2,0:T(4,128)S(1)}, u32[]{:S(2)}) copy-start(f32[16,8,3]{1,2,0:T(4,128)S(1)} %all-gather.4) | copy-start | bytes 4612
  90.5 6.3 %copy-start.7 = (f32[16,8,3]{1,2,0:T(4,128)}, f32[16,8,3]{1,2,0:T(4,128)S(1)}, u32[]{:S(2)}) copy-start(f32[16,8,3]{1,2,0:T(4,128)S(1)} %all-gather.3) | copy-start | bytes 4612
  90.5 6.2 %copy-start.9 = (bf16[104,3,64]{2,1,0:T(4,128)(2,1)S(1)}, bf16[104,3,64]{2,1,0:T(4,128)(2,1)}, u32[]{:S(2)}) copy-start(bf16[104,3,64]{2,1,0:T(4,128)(2,1)} %copy-done.8) | copy-start | bytes 119812
  90.5 6.2 %copy-start.11 = (bf16[104,3,64]{2,1,0:T(4,128)(2,1)S(1)}, bf16[104,3,64]{2,1,0:T(4,128)(2,1)}, u32[]{:S(2)}) copy-start(bf16[104,3,64]{2,1,0:T(4,128)(2,1)} %copy-done.10) | copy-start | bytes 119812
  98.8 1.1 slice-start
  98.8 1.1 slice-start.1
  109.1 59.6 %copy-start.5 = (bf16[8,3072]{1,0:T(8,128)(2,1)S(1)}, bf16[8,3072]{1,0:T(8,128)(2,1)}, u32[]{:S(2)}) copy-start(bf16[8,3072]{1,0:T(8,128)(2,1)} %param.14) | copy-start | bytes 147460
Sparse Core Ops, SparseCore 0:
  106.3 62.3 all-reduce.1
where the time goes:
time: 179 us
  blocking collectives  69.3 us (39%)
  waiting for transfers between devices  52.1 us (29%)
  other arithmetic  29 us (16%)
  between operations  14.5 us (8%)
  matrix products  8.79 us (5%)
  local copies, waits for them, and re-layouts  4.56 us (3%)
    all_gather x3, blocking collectives, merged(): pieces = jax.tree.map(lambda part: lax.all_gather(part, axis), value)  69.3 us
    psum x1, waiting for transfers between devices, per_device(): summed_heads = lax.psum(head_terms, 'tp')  52.1 us
    unnamed x2, other arithmetic  10.5 us
    select_n x1, other arithmetic, per_device(): jnp.where(short_write[:, None, :, None], fresh[:short_count, :, None, :],...  6.17 us
  transfers between devices with their start and end apart: 1, of which 1 were waited for; matrix products, arithmetic and copies ran while one was open for 6% of the time, Pallas kernels for 0%

commit v1 on v0

--- a/solution.py
+++ b/solution.py
@@ -1,3 +1,4 @@
+import functools
 import jax
 import jax.numpy as jnp
 from jax import lax
@@ -5,6 +6,20 @@
 
 rope_theta = 500000.0
 floor_score = -1e30
+
+
+def extend_the_skins(row_data, bus_axis):
+    total_devices = lax.axis_size(bus_axis)
+    x_next = row_data
+    for w in [
+        [(h, h ^ j) for h in range(total_devices)] for j in (1, 2, 4, 8, 16) if j < total_devices
+    ]:
+        shaped = lax.ppermute(x_next, bus_axis, perm=w)
+        x_next = x_next + shaped
+    return x_next
+
+
+launch_indices = functools.partial(extend_the_skins, bus_axis="tp")
 
 
 def merged(value, axis, join):
@@ -141,7 +156,7 @@
         [short_mix.reshape(short_count, -1), long_mix.reshape(long_count, -1)], axis=0
     ).astype(jnp.bfloat16)
     head_terms = jnp.dot(mixed, w_out, preferred_element_type=jnp.float32)
-    summed_heads = lax.psum(head_terms, "tp")
+    summed_heads = launch_indices(head_terms)
     hidden = (residual + summed_heads).astype(jnp.bfloat16)
     return (hidden[:short_count], hidden[short_count:], short_out, long_out)
 

time: 179 us -> 166 us (0.927)
  between operations: 14.5 us -> 1.09 us
  other arithmetic: 29 us -> 23.5 us
  starting transfers between devices: 0.04 us -> 4.76 us
    ppermute x0 -> x3, waiting for transfers between devices: none -> 53.4 us  [extend_the_skins(): shaped = lax.ppermute(x_next, bus_axis, perm=w)]
    psum x1 -> x0, waiting for transfers between devices: 52.1 us -> none  [per_device(): summed_heads = lax.psum(head_terms, 'tp')]
    ppermute x0 -> x3, starting transfers between devices: none -> 4.76 us  [extend_the_skins(): shaped = lax.ppermute(x_next, bus_axis, perm=w)]
    unnamed x2 -> x3, other arithmetic: 10.5 us -> 5.97 us
  transfers between devices with their start and end apart: 1 -> 3, of which waited for: 1 -> 3; matrix products, arithmetic and copies ran while one was open for 6% -> 4% of each run, Pallas kernels for 0% -> 0%
where the time goes in v1:
time: 166 us; the launch traced here: 165 us
  blocking collectives  69.3 us (42%)
  waiting for transfers between devices  53.4 us (32%)
  other arithmetic  23.5 us (14%)
  matrix products  7.72 us (5%)
  local copies, waits for them, and re-layouts  5.02 us (3%)
  starting transfers between devices  4.76 us (3%)
    all_gather x3, blocking collectives, merged(): pieces = jax.tree.map(lambda part: lax.all_gather(part, axis), value)  69.3 us
    ppermute x3, waiting for transfers between devices, extend_the_skins(): shaped = lax.ppermute(x_next, bus_axis, perm=w)  53.4 us
    select_n x1, other arithmetic, per_device(): jnp.where(short_write[:, None, :, None], fresh[:short_count, :, None, :],...  6.17 us
    unnamed x3, other arithmetic  5.97 us
    ppermute x3, starting transfers between devices, extend_the_skins(): shaped = lax.ppermute(x_next, bus_axis, perm=w)  4.76 us
  transfers between devices with their start and end apart: 3, of which 3 were waited for; matrix products, arithmetic and copies ran while one was open for 4% of the time, Pallas kernels for 0%

profile of v1, /device:TPU:0, one launch (start us, length us, event | category | flops | bytes accessed | tf_op | source)
XLA Modules:
  0.0 165.0 jit_solution(15543542011339521063)
XLA Ops:
  0.7 0.8 convert_element_type.43
  1.5 1.3 fusion.7
  2.8 0.7 iota_compare_fusion.1
  3.6 0.8 add_convert_fusion.1
  4.3 0.9 multiply_cosine_fusion.1
  5.2 1.8 %convolution_bitcast_fusion = f32[104,1,128]{2,0,1:T(8,128)S(1)} fusion(bf16[3072,128]{1,0:T(8,128)(2,1)} %param.17, f32[3072]{0:T(1024)S(1)} %convert_element_type.43, f32[104]{0:T(128)S(1)} %add_rsqrt_fusion, bf16[8,3072]{1,0:T(8,128)(2,1)} %param.14, bf16[96,3072]{1,0:T(8,128)(2,1)} %param.13), kind=kOutput, calls=%fused_computation.33 | convolution fusion | flops 84025344 | bytes 1491360 | tf_op jit(solution)/shard_map/dot_general | solution.py:90
  7.1 0.3 fusion.30
  7.4 0.4 fusion.18
  7.8 0.7 pad_maximum_fusion.2
  8.6 0.5 copy-done.13
  9.1 1.1 fusion.43
  10.2 0.1 copy.64
  10.4 0.1 copy.65
  10.5 0.7 broadcast_compare_fusion.1
  11.2 1.9 %bitcast_select_fusion.1 = bf16[8,1,512,256]{3,2,0,1:T(8,128)(2,1)S(1)} fusion(bf16[8,1,512,256]{3,2,1,0:T(8,128)(2,1)} %param.23, pred[8,512]{1,0:T(8,128)(4,1)S(1)} %get-tuple-element.102, bf16[8,256]{1,0:T(8,128)(2,1)S(1)} %maximum_bitcast_fusion), kind=kLoop, calls=%fused_computation.17 | loop fusion | flops 1048576 | bytes 4202496 | tf_op jit(solution)/shard_map/jit(_where)/select_n | solution.py:130
  13.2 0.1 subtract_convert_fusion
  13.4 0.5 fusion.47
  13.8 0.6 fusion.19
  14.5 25.5 %all-gather.2 = f32[128,3,128]{2,0,1:T(8,128)S(1)} all-gather(f32[8,3,128]{2,0,1:T(8,128)S(1)} %copy.51), channel_id=4, replica_groups=mesh['req'=16,'tp'=8] {'req'}, dimensions={0}, use_global_device_ids=true | all-gather | bytes 208896 | tf_op jit(solution)/shard_map/all_gather | solution.py:26
  40.0 0.2 fusion.33
  40.2 0.1 copy.50
  40.2 22.8 %all-gather.4 = f32[16,8,3]{1,2,0:T(4,128)S(1)} all-gather(f32[1,8,3]{1,2,0:T(4,128)S(1)} %bitcast.104), channel_id=3, replica_groups=mesh['req'=16,'tp'=8] {'req'}, dimensions={0}, use_global_device_ids=true | all-gather | bytes 1632 | tf_op jit(solution)/shard_map/all_gather | solution.py:26
  63.1 0.1 copy.49
  63.2 21.1 %all-gather.3 = f32[16,8,3]{1,2,0:T(4,128)S(1)} all-gather(f32[1,8,3]{1,2,0:T(4,128)S(1)} %bitcast.105), channel_id=2, replica_groups=mesh['req'=16,'tp'=8] {'req'}, dimensions={0}, use_global_device_ids=true | all-gather | bytes 1632 | tf_op jit(solution)/shard_map/all_gather | solution.py:26
  84.3 6.2 %bitcast_select_fusion = bf16[96,1,128,256]{3,2,0,1:T(8,128)(2,1)S(1)} fusion(bf16[96,1,128,256]{3,2,1,0:T(8,128)(2,1)} %param.22, pred[96,128]{1,0:T(8,128)(4,1)S(1)} %get-tuple-element.106, bf16[96,256]{1,0:T(8,128)(2,1)S(1)} %slice_bitcast_fusion.15), kind=kLoop, calls=%fused_computation.12 | loop fusion | flops 3145728 | bytes 12644352 | tf_op jit(solution)/shard_map/jit(_where)/select_n | solution.py:103
  90.5 1.8 %fusion.15 = f32[96,3,128]{2,1,0:T(4,128)S(1)} fusion(bf16[96,1,128,256]{3,2,0,1:T(8,128)(2,1)S(1)} %bitcast_select_fusion, pred[96,128]{1,0:T(8,128)(4,1)S(1)} %get-tuple-element.105, bf16[104,3,64]{2,1,0:T(4,128)(2,1)S(1)} %copy-done.12, bf16[104,3,64]{2,1,0:T(4,128)(2,1)S(1)} %copy-done.10), kind=kOutput, calls=%fused_computation.29 | convolution fusion | flops 9670656 | bytes 3518464 | tf_op jit(solution)/shard_map/rkgd,rksd->rkgs/dot_general | solution.py:107
  92.3 0.3 fusion.48
  92.6 1.0 fusion.16
  93.7 4.6 %while.14 = (s32[]{:T(128)}, f32[8,1,3]{0,1,2:T(1,128)S(1)}, f32[8,1,3]{0,1,2:T(1,128)S(1)}, f32[8,1,3,128]{3,2,1,0:T(4,128)S(1)}, f32[15,8,1,3]{1,0,3,2:T(8,128...) while((s32[]{:T(128)}, f32[8,1,3]{0,1,2:T(1,128)S(1)}, ...), condition=%wide.region_6.7_spmd, body=%wide.region_5.6_spmd.sunk | while | flops 9362 | bytes 62877 | solution.py:29
  93.7 0.1 copy.85
  93.9 0.1 fusion.59
  94.0 0.1 copy.85
  94.2 0.1 fusion.59
  94.3 0.1 copy.85
  94.5 0.1 fusion.59
  94.6 0.1 copy.85
  94.8 0.1 fusion.59
  94.9 0.1 copy.85
  95.1 0.1 fusion.59
  95.3 0.1 copy.85
  95.4 0.1 fusion.59
  95.7 0.1 fusion.59
  96.0 0.1 fusion.59
  96.3 0.1 fusion.59
  96.6 0.1 fusion.59
  97.0 0.1 fusion.59
  97.3 0.1 fusion.59
  97.6 0.1 fusion.59
  97.9 0.1 fusion.59
  98.2 0.1 fusion.59
  98.4 0.5 fusion.21
  98.9 0.1 collective-permute-start
  99.0 3.0 %collective-permute-done = f32[104,3072]{1,0:T(8,128)S(1)} collective-permute-done((f32[104,3072]{1,0:T(8,128)S(1)}, f32[104,3072]{1,0:T(8,128)S(1)}, u32[]{:S(2)}, u32[]{:S(2)}) %collective-permute-start) | collective-permute-done | bytes 1277984 | tf_op jit(solution)/shard_map/ppermute | solution.py:17
  102.0 0.1 add.54
  102.1 1.6 collective-permute-start.1
  103.7 28.6 %collective-permute-done.1 = f32[104,3072]{1,0:T(8,128)S(1)} collective-permute-done((f32[104,3072]{1,0:T(8,128)S(1)}, f32[104,3072]{1,0:T(8,128)S(1)}, u32[]{:S(2)}, u32[]{:S(2)}) %collective-permute-start.1) | collective-permute-done | bytes 1277984 | tf_op jit(solution)/shard_map/ppermute | solution.py:17
  132.3 0.1 add.55
  132.5 3.1 %collective-permute-start.2 = (f32[104,3072]{1,0:T(8,128)S(1)}, f32[104,3072]{1,0:T(8,128)S(1)}, u32[]{:S(2)}, u32[]{:S(2)}) collective-permute-start(f32[104,3072]{1,0:T(8,128)S(1)} %add.55), channel_id=1, source_target_pairs={{0,4},{1,5},{2,6},{3,7},{4,0},{5,1},{6,2},{7,3},{8,12},{9,13},{10,... | collective-permute-start | bytes 3833864 | tf_op jit(solution)/shard_map/ppermute | solution.py:17
  135.6 1.7 %fusion.54 = bf16[8,1,512,256]{3,2,1,0:T(8,128)(2,1)} fusion(bf16[8,1,512,256]{3,2,1,0:T(8,128)(2,1)S(1)} %copy-done.1, bf16[8,256]{1,0:T(8,128)(2,1)S(1)} %maximum_bitcast_fusion, pred[8,512]{1,0:T(8,128)(4,1)S(1)} %get-tuple-element.102), kind=kLoop, calls=%fused_computation.92 | loop fusion | flops 1048576 | bytes 4202496
  137.3 4.3 %fusion.55 = bf16[96,1,128,256]{3,2,1,0:T(8,128)(2,1)} fusion(bf16[96,1,128,256]{3,2,1,0:T(8,128)(2,1)S(1)} %bitcast.97, bf16[96,256]{1,0:T(8,128)(2,1)S(1)} %slice_bitcast_fusion.15, pred[96,128]{1,0:T(8,128)(4,1)S(1)} %get-tuple-element.106), kind=kLoop, calls=%fused_computation.93 | loop fusion | flops 3145728 | bytes 12644352
  141.6 21.8 %collective-permute-done.2 = f32[104,3072]{1,0:T(8,128)S(1)} collective-permute-done((f32[104,3072]{1,0:T(8,128)S(1)}, f32[104,3072]{1,0:T(8,128)S(1)}, u32[]{:S(2)}, u32[]{:S(2)}) %collective-permute-start.2) | collective-permute-done | bytes 1277984 | tf_op jit(solution)/shard_map/ppermute | solution.py:17
  163.3 0.2 fusion.10
  163.6 0.9 slice.107
  164.4 0.6 slice.108
  (111 shorter events, 2.8 us)
Async XLA Ops:
  0.6 97.7 %copy-start = (bf16[384,3072]{1,0:T(8,128)(2,1)S(1)}, bf16[384,3072]{1,0:T(8,128)(2,1)}, u32[]{:S(2)}) copy-start(bf16[384,3072]{1,0:T(8,128)(2,1)} %param.19) | copy-start | bytes 7077892
  5.2 2.1 %copy-start.2 = (bf16[96,3072]{1,0:T(8,128)(2,1)S(1)}, bf16[96,3072]{1,0:T(8,128)(2,1)}, u32[]{:S(2)}) copy-start(bf16[96,3072]{1,0:T(8,128)(2,1)} %param.13) | copy-start | bytes 1769476
  5.2 2.1 %copy-start.5 = (bf16[8,3072]{1,0:T(8,128)(2,1)S(1)}, bf16[8,3072]{1,0:T(8,128)(2,1)}, u32[]{:S(2)}) copy-start(bf16[8,3072]{1,0:T(8,128)(2,1)} %param.14) | copy-start | bytes 147460
  5.2 2.1 %copy-start.14 = (bf16[3072,128]{1,0:T(8,128)(2,1)S(1)}, bf16[3072,128]{1,0:T(8,128)(2,1)}, u32[]{:S(2)}) copy-start(bf16[3072,128]{1,0:T(8,128)(2,1)} %param.18) | copy-start | bytes 2359300
  7.4 1.7 %copy-start.13 = (bf16[3072,384]{1,0:T(8,128)(2,1)S(1)}, bf16[3072,384]{1,0:T(8,128)(2,1)}, u32[]{:S(2)}) copy-start(bf16[3072,384]{1,0:T(8,128)(2,1)} %param.16) | copy-start | bytes 7077892
  11.2 2.0 %copy-start.3 = (f32[104,64]{1,0:T(8,128)S(1)}, f32[104,64]{1,0:T(8,128)}, u32[]{:S(2)}) copy-start(f32[104,64]{1,0:T(8,128)} %get-tuple-element.104) | copy-start | bytes 79876
  13.3 1.1 copy-start.9
  13.3 1.1 copy-start.11
  13.8 70.4 %copy-start.4 = (bf16[104,1,256]{2,0,1:T(8,128)(2,1)S(1)}, bf16[104,1,256]{2,0,1:T(8,128)(2,1)}, u32[]{:S(2)}) copy-start(bf16[104,1,256]{2,0,1:T(8,128)(2,1)} %pad_maximum_fusion.2) | copy-start | bytes 159748
  63.0 27.4 %copy-start.7 = (f32[16,8,3]{1,2,0:T(4,128)}, f32[16,8,3]{1,2,0:T(4,128)S(1)}, u32[]{:S(2)}) copy-start(f32[16,8,3]{1,2,0:T(4,128)S(1)} %all-gather.4) | copy-start | bytes 4612
  84.2 6.3 %copy-start.8 = (f32[16,8,3]{1,2,0:T(4,128)}, f32[16,8,3]{1,2,0:T(4,128)S(1)}, u32[]{:S(2)}) copy-start(f32[16,8,3]{1,2,0:T(4,128)S(1)} %all-gather.3) | copy-start | bytes 4612
  84.3 6.2 %copy-start.10 = (bf16[104,3,64]{2,1,0:T(4,128)(2,1)S(1)}, bf16[104,3,64]{2,1,0:T(4,128)(2,1)}, u32[]{:S(2)}) copy-start(bf16[104,3,64]{2,1,0:T(4,128)(2,1)} %copy-done.9) | copy-start | bytes 119812
  84.3 6.2 %copy-start.12 = (bf16[104,3,64]{2,1,0:T(4,128)(2,1)S(1)}, bf16[104,3,64]{2,1,0:T(4,128)(2,1)}, u32[]{:S(2)}) copy-start(bf16[104,3,64]{2,1,0:T(4,128)(2,1)} %copy-done.11) | copy-start | bytes 119812
  92.6 1.1 slice-start.2
  92.6 1.1 slice-start.3
  98.9 3.1 %collective-permute-start = (f32[104,3072]{1,0:T(8,128)S(1)}, f32[104,3072]{1,0:T(8,128)S(1)}, u32[]{:S(2)}, u32[]{:S(2)}) collective-permute-start(f32[104,3072]{1,0:T(8,128)S(1)} %fusion.21), channel_id=1, source_target_pairs={{0,1},{1,0},{2,3},{3,2},{4,5},{5,4},{6,7},{7,6},{8,9},{9,8},{10,11... | collective-permute-start | bytes 3833864 | tf_op jit(solution)/shard_map/ppermute | solution.py:17
  102.0 33.6 %copy-start.1 = (bf16[8,1,512,256]{3,2,1,0:T(8,128)(2,1)S(1)}, bf16[8,1,512,256]{3,2,1,0:T(8,128)(2,1)}, u32[]{:S(2)}) copy-start(bf16[8,1,512,256]{3,2,1,0:T(8,128)(2,1)} %param.23) | copy-start | bytes 6291460
  102.0 35.3 %slice-start = ((s8[6291456]{0:T(1024)(128)(4,1)}), s8[4194304]{0:T(1024)(128)(4,1)S(1)}, s32[]{:S(2)}) async-start(s8[6291456]{0:T(1024)(128)(4,1)} %bitcast.96), calls=%async_computation | async-start | bytes 8388608
  102.1 35.1 %slice-start.1 = ((s8[6291456]{0:T(1024)(128)(4,1)}), s8[2097152]{0:T(1024)(128)(4,1)S(1)}, s32[]{:S(2)}) async-start(s8[6291456]{0:T(1024)(128)(4,1)} %bitcast.96), calls=%async_computation.1 | async-start | bytes 4194304
  102.1 30.2 %collective-permute-start.1 = (f32[104,3072]{1,0:T(8,128)S(1)}, f32[104,3072]{1,0:T(8,128)S(1)}, u32[]{:S(2)}, u32[]{:S(2)}) collective-permute-start(f32[104,3072]{1,0:T(8,128)S(1)} %add.54), channel_id=1, source_target_pairs={{0,2},{1,3},{2,0},{3,1},{4,6},{5,7},{6,4},{7,5},{8,10},{9,11},{10,... | collective-permute-start | bytes 3833864 | tf_op jit(solution)/shard_map/ppermute | solution.py:17
  132.5 30.8 %collective-permute-start.2 = (f32[104,3072]{1,0:T(8,128)S(1)}, f32[104,3072]{1,0:T(8,128)S(1)}, u32[]{:S(2)}, u32[]{:S(2)}) collective-permute-start(f32[104,3072]{1,0:T(8,128)S(1)} %add.55), channel_id=1, source_target_pairs={{0,4},{1,5},{2,6},{3,7},{4,0},{5,1},{6,2},{7,3},{8,12},{9,13},{10,... | collective-permute-start | bytes 3833864 | tf_op jit(solution)/shard_map/ppermute | solution.py:17
  137.3 26.1 %copy-start.6 = (bf16[8,3072]{1,0:T(8,128)(2,1)S(1)}, bf16[8,3072]{1,0:T(8,128)(2,1)}, u32[]{:S(2)}) copy-start(bf16[8,3072]{1,0:T(8,128)(2,1)} %param.14) | copy-start | bytes 147460
